TPU v7x, 256 devices: a whole 4x4x8 slice. The times are simulated.
256 devices in a mesh: order: 16 (over x_hi, z), blk: 16 (over y, x_lo, core).
Axes of the slice: x: 4 (x_hi: 2, x_lo: 2; x = x_hi * 2 + x_lo), y: 4, z: 8, core: 2. Of those that a mesh axis runs over, the one named last changes fastest.
Arguments:
- fourier_cycles: float32 [32, 512, 128], P('order', 'blk'), parts along dimension 0, may hold values from -6 to 6
- legendre: float32 [32, 512, 12288], P('order', 'blk'), parts along dimension 0, may hold values from -0.25 to 0.25
- cycle_weight: float32 [512], P('blk'), may hold values from 0.5 to 2
- matched_filter_weights: float32 [12288, 8, 8], P('blk'), may hold values from -2 to 2
- cluster_cycles: int32 [32, 64], P('order'), parts along dimension 0, may hold values from 0 to 511
- cluster_flux: float32 [32, 64, 128], P('order'), parts along dimension 0, may hold values from -18 to 18
- order_per_slot: int32 [32], P('order'), parts along dimension 0, may hold values from 0 to 6143
Outputs:
- synthesized: float32 [32, 512, 128], P('order', 'blk'), parts along dimension 0
There are 16 independent parts, one for each index of `order`. A program takes and returns all parts, laid end to end along the dimension named above; an argument that names none is the same for every part. Nothing has to cross between parts.
Inputs may be any that keep to these rules, and one draw needn't show every extreme that they name: `cluster_cycles`: cycle indices; several clusters may share a cycle, and their coefficients add. `order_per_slot`: order of each slot; degrees below it carry no coefficients.
All inputs are finite; a program needn't handle non-finite values.
Results may differ from a plain program's by a relative error of at most 0.00011.
Values sent between devices are 32-bit elements; how exact they have to be, the bound alone decides.
A program may use at most 128 MiB of HBM per device.

v0:
```python
import jax
import jax.numpy as jnp
from jax import lax
from jax.sharding import PartitionSpec as P

L = 12288
F = 8
S = 8
SIMS = 8
M = 2
highest_degree = lax.Precision.HIGHEST


def inject(fourier_cycles, cycle_weight, cluster_cycles, cluster_flux):
    local = fourier_cycles.shape[1]
    cycle_ids = lax.axis_index("blk") * local + lax.iota(jnp.int32, local)
    cycle_hits = (cycle_ids[None, :, None] == cluster_cycles[:, None, :]).astype(jnp.float32)
    added = jnp.einsum("krj,kjc->krc", cycle_hits, cluster_flux, precision=highest_degree)
    return cycle_weight[None, :, None] * (fourier_cycles + added)


def finish(owned, matched_filter_weights, order_per_slot):
    blocks = owned.shape[0]
    degrees = lax.axis_index("blk") * blocks + lax.iota(jnp.int32, blocks)
    harmonics = owned.reshape(blocks, M, 2 * F * SIMS)
    kept_mask = (degrees[:, None] >= order_per_slot[None, :]).astype(jnp.float32)
    masked_values = (harmonics * kept_mask[:, :, None]).reshape(blocks, M, 2, F, SIMS)
    matched_output = jnp.einsum(
        "dvr,dotrq->dotvq", matched_filter_weights, masked_values, precision=highest_degree
    )
    squares = jnp.sum(matched_filter_weights * matched_filter_weights, axis=2)
    weights = kept_mask * (2.0 * degrees.astype(jnp.float32) + 1.0)[:, None]
    response = jnp.einsum("lk,ls->ks", weights, squares, precision=highest_degree)
    response = lax.psum(response, "blk")
    scaled = matched_output * (L / jnp.sqrt(response))[None, :, None, :, None]
    return scaled.reshape(blocks, M, 2 * S * SIMS)


def body(
    fourier_cycles,
    legendre,
    cycle_weight,
    matched_filter_weights,
    cluster_cycles,
    cluster_flux,
    order_per_slot,
):
    injected = inject(fourier_cycles, cycle_weight, cluster_cycles, cluster_flux)
    orders_here = legendre.shape[0]
    width = injected.shape[2]
    blocks = legendre.shape[2] // lax.axis_size("blk")
    columns = legendre
    partial_running_sum = jnp.einsum("krl,krc->lkc", columns, injected, precision=highest_degree)
    owned = lax.psum_scatter(
        partial_running_sum.reshape(blocks * lax.axis_size("blk"), orders_here * width),
        "blk",
        scatter_dimension=0,
        tiled=True,
    )
    scaled = finish(owned, matched_filter_weights, order_per_slot)
    columns = legendre
    return jnp.einsum(
        "krl,lkc->krc",
        columns,
        lax.all_gather(scaled, "blk", axis=0, tiled=True),
        precision=highest_degree,
    )


def solution(mesh):
    return jax.shard_map(
        body,
        mesh=mesh,
        in_specs=(
            P("order", "blk", None),
            P("order", "blk", None),
            P("blk"),
            P("blk", None, None),
            P("order", None),
            P("order", None, None),
            P("order"),
        ),
        out_specs=P("order", "blk", None),
        check_vma=False,
    )
```

profile of v0, /device:TPU:1, one launch (start us, length us, event | category | flops | bytes accessed | tf_op | source)
XLA Modules:
  0.0 300.5 jit_solution(4388038787292911202)
XLA Ops:
  6.5 0.0 copy-start
  6.5 0.0 reduce-scatter.2.cloned.1.call-start
  6.5 1.2 fusion
  7.7 0.8 copy-done
  8.5 0.0 copy-start.2
  8.5 12.6 %fusion.10 = f32[2,128,12288]{2,1,0:T(8,128)} fusion(f32[2,32,128]{2,1,0:T(8,128)S(1)} %fusion, f32[2,32,12288]{2,1,0:T(8,128)S(1)} %copy-done), kind=kOutput, calls=%fused_computation.21 | convolution fusion | flops 1207959552 | bytes 15761408 | tf_op jit(solution)/shard_map/krl,krc->lkc/dot_general | solution.py:53
  21.1 0.0 reduce-scatter.2.cloned.1.call-update
  21.1 0.0 all-gather.2.cloned.1.call-start
  21.1 0.0 copy-done.1
  21.2 2.3 copy.17
  23.5 0.1 multiply_reduce_fusion
  23.5 0.0 copy-done.2
  23.5 0.2 fusion.4
  23.7 30.7 %psum.7 = f32[2,8]{1,0:T(2,128)S(1)} all-reduce(f32[2,8]{1,0:T(2,128)S(1)} %fusion.4), channel_id=1, replica_groups=mesh['order'=16,'blk'=16] {'blk'}, use_global_device_ids=true, to_apply=%region_2.0 | all-reduce | flops 16 | bytes 128 | tf_op jit(solution)/shard_map/psum | solution.py:34
  54.5 0.1 compare_convert_fusion
  54.5 111.8 %reduce-scatter.2.cloned.1.call-done = f32[768,256]{0,1:T(8,128)} async-done(((f32[12288,256]{0,1:T(8,128)}), f32[768,256]{0,1:T(8,128)}) %reduce-scatter.2.cloned.1.call-update) | async-done | bytes 786448 | tf_op jit(solution)/shard_map/reduce_scatter | solution.py:54
  166.3 2.1 broadcast_multiply_fusion
  168.4 11.3 %copy.13 = f32[768,2,2,8,8]{3,4,2,1,0:T(8,128)} copy(f32[768,2,2,8,8]{0,4,3,2,1:T(8,128)} %broadcast_multiply_fusion) | data formatting | bytes 1572864 | tf_op jit(solution)/shard_map/mul | solution.py:27
  179.8 16.1 %multiply_bitcast_fusion = f32[768,2,2,8,8]{3,4,2,1,0:T(8,128)} fusion(f32[2,8]{1,0:T(2,128)S(1)} %rsqrt_multiply_fusion, f32[768,2,2,8,8]{3,4,2,1,0:T(8,128)} %copy.13, f32[768,8,8,1,1]{2,1,4,3,0:T(8,128)} %copy.17), kind=kOutput, calls=%fused_computation | convolution fusion | flops 19070976 | bytes 1769536 | tf_op jit(solution)/shard_map/dvr,dotrq->dotvq/dot_general | solution.py:28
  195.8 9.9 %copy.15 = f32[768,2,2,8,8]{0,4,3,2,1:T(8,128)} copy(f32[768,2,2,8,8]{3,4,2,1,0:T(8,128)} %multiply_bitcast_fusion) | data formatting | bytes 1572864 | tf_op jit(solution)/shard_map/mul | solution.py:35
  205.8 2.3 copy.16
  208.1 0.0 all-gather.2.cloned.1.call-update
  208.1 75.4 %all-gather.2.cloned.1.call-done = f32[12288,2,128]{2,0,1:T(8,128)} async-done(((f32[768,2,128]{2,0,1:T(8,128)}), f32[12288,2,128]{2,0,1:T(8,128)}) %all-gather.2.cloned.1.call-update) | async-done | bytes 12582928 | tf_op jit(solution)/shard_map/all_gather | solution.py:65
  283.5 10.2 %convolution_bitcast_fusion = f32[2,32,128]{2,1,0:T(8,128)} fusion(f32[12288,2,128]{2,0,1:T(8,128)} %all-gather.2.cloned.1.call-done, f32[2,32,12288]{2,1,0:T(8,128)S(1)} %copy-done), kind=kOutput, calls=%fused_computation.1 | convolution fusion | flops 1207959552 | bytes 15761408 | tf_op jit(solution)/shard_map/krl,lkc->krc/dot_general | solution.py:62
  (5 shorter events, 0.0 us)
Async XLA Ops:
  6.5 2.0 copy-start
  6.5 159.8 %reduce-scatter.2.cloned.1.call-start = ((), (), s32[]{:S(2)}) async-start(), calls=%async_computation.1 | async-start | bytes 13369344 | tf_op jit(solution)/shard_map/reduce_scatter | solution.py:54
  8.5 12.6 %copy-start.1 = (f32[768,8,8]{0,2,1:T(8,128)S(1)}, f32[768,8,8]{0,2,1:T(8,128)}, u32[]{:S(2)}) copy-start(f32[768,8,8]{0,2,1:T(8,128)} %param.10) | copy-start | bytes 589828
  8.5 15.0 %copy-start.2 = (s32[2]{0:T(128)S(1)}, s32[2]{0:T(128)}, u32[]{:S(2)}) copy-start(s32[2]{0:T(128)} %param.13) | copy-start | bytes 28
  21.1 262.4 %all-gather.2.cloned.1.call-start = ((), (), s32[]{:S(2)}) async-start(), calls=%async_computation.2 | async-start | bytes 13369344 | tf_op jit(solution)/shard_map/all_gather | solution.py:65
Sparse Core Ops, SparseCore 0:
  21.2 145.0 reduce-scatter.1
  208.2 75.2 all-gather.1
where the time goes:
time: 301 us
  waiting for transfers between devices  187 us (62%)
  matrix products  40.3 us (13%)
  blocking collectives  30.7 us (10%)
  local copies, waits for them, and re-layouts  26.6 us (9%)
  between operations  13.4 us (4%)
    reduce_scatter x1, waiting for transfers between devices, body(): lax.psum_scatter(partial_running_sum.reshape(blocks * lax.axis_size('blk'...  112 us
    all_gather x1, waiting for transfers between devices, body(): lax.all_gather(scaled, 'blk', axis=0, tiled=True)  75.4 us
    psum x1, blocking collectives, finish(): response = lax.psum(response, 'blk')  30.7 us
    dot_general x1, matrix products, finish(): jnp.einsum('dvr,dotrq->dotvq', matched_filter_weights, masked_values, pre...  16.1 us
    dot_general x1, matrix products, body(): jnp.einsum('krl,krc->lkc', columns, injected, precision=highest_degree)  12.6 us
    mul x1, local copies, waits for them, and re-layouts, finish(): harmonics * kept_mask[:, :, None]  11.3 us
    dot_general x1, matrix products, body(): jnp.einsum('krl,lkc->krc', columns, lax.all_gather(scaled, 'blk', axis=0,...  10.2 us
    mul x1, local copies, waits for them, and re-layouts, finish(): scaled = matched_output * (L / jnp.sqrt(response))[None, :, None, :, None]  9.92 us
  transfers between devices with their start and end apart: 2, of which 2 were waited for; matrix products, arithmetic and copies ran while one was open for 1% of the time, Pallas kernels for 0%

commit v1 on v0

--- a/solution.py
+++ b/solution.py
@@ -62,7 +62,9 @@
     return jnp.einsum(
         "krl,lkc->krc",
         columns,
-        lax.all_gather(scaled, "blk", axis=0, tiled=True),
+        jnp.concatenate(
+            lax.all_to_all(jnp.stack([scaled] * lax.axis_size("blk")), "blk", 0, 0), axis=0
+        ),
         precision=highest_degree,
     )
 

time: 301 us -> 383 us (1.27)
  blocking collectives: 30.7 us -> 175 us
  waiting for transfers between devices: 187 us -> 112 us
  local copies, waits for them, and re-layouts: 26.6 us -> 39.5 us
    all_to_all x0 -> x1, blocking collectives: none -> 145 us  [body(): lax.all_to_all(jnp.stack([scaled] * lax.axis_size('blk')), 'blk', 0, 0)]
    all_gather x1 -> x0, waiting for transfers between devices: 75.4 us -> none  [body(): lax.all_gather(scaled, 'blk', axis=0, tiled=True)]
    all_to_all x0 -> x1, local copies, waits for them, and re-layouts: none -> 10.4 us  [body(): lax.all_to_all(jnp.stack([scaled] * lax.axis_size('blk')), 'blk', 0, 0)]
    another operation x0 -> x2, local copies, waits for them, and re-layouts: none -> 4.85 us  [body(): jnp.stack([scaled] * lax.axis_size('blk'))]
  transfers between devices with their start and end apart: 2 -> 1, of which waited for: 2 -> 1; matrix products, arithmetic and copies ran while one was open for 1% -> 1% of each run, Pallas kernels for 0% -> 0%
where the time goes in v1:
time: 383 us
  blocking collectives  175 us (46%)
  waiting for transfers between devices  112 us (29%)
  matrix products  40.2 us (10%)
  local copies, waits for them, and re-layouts  39.5 us (10%)
  between operations  13.4 us (3%)
    all_to_all x1, blocking collectives, body(): lax.all_to_all(jnp.stack([scaled] * lax.axis_size('blk')), 'blk', 0, 0)  145 us
    reduce_scatter x1, waiting for transfers between devices, body(): lax.psum_scatter(partial_running_sum.reshape(blocks * lax.axis_size('blk'...  112 us
    psum x1, blocking collectives, finish(): response = lax.psum(response, 'blk')  30.5 us
    dot_general x1, matrix products, finish(): jnp.einsum('dvr,dotrq->dotvq', matched_filter_weights, masked_values, pre...  16.1 us
    dot_general x1, matrix products, body(): jnp.einsum('krl,krc->lkc', columns, injected, precision=highest_degree)  12.4 us
    mul x1, local copies, waits for them, and re-layouts, finish(): harmonics * kept_mask[:, :, None]  11.3 us
    all_to_all x1, local copies, waits for them, and re-layouts, body(): lax.all_to_all(jnp.stack([scaled] * lax.axis_size('blk')), 'blk', 0, 0)  10.4 us
    dot_general x1, matrix products, body(): jnp.einsum('krl,lkc->krc', columns, jnp.concatenate(lax.all_to_all(jnp.st...  10.2 us
  transfers between devices with their start and end apart: 1, of which 1 were waited for; matrix products, arithmetic and copies ran while one was open for 1% of the time, Pallas kernels for 0%

profile of v1, /device:TPU:1, one launch (start us, length us, event | category | flops | bytes accessed | tf_op | source)
XLA Modules:
  0.0 382.6 jit_solution(14891296175810559527)
XLA Ops:
  6.5 0.0 copy-start
  6.5 0.0 reduce-scatter.2.cloned.1.call-start
  6.5 1.2 fusion
  7.7 0.8 copy-done
  8.5 0.0 copy-start.2
  8.5 12.4 %fusion.10 = f32[2,128,12288]{2,1,0:T(8,128)} fusion(f32[2,32,128]{2,1,0:T(8,128)S(1)} %fusion, f32[2,32,12288]{2,1,0:T(8,128)S(1)} %copy-done), kind=kOutput, calls=%fused_computation.21 | convolution fusion | flops 1207959552 | bytes 15761408 | tf_op jit(solution)/shard_map/krl,krc->lkc/dot_general | solution.py:53
  20.9 0.0 reduce-scatter.2.cloned.1.call-update
  21.0 0.0 copy-done.1
  21.0 2.3 copy.18
  23.3 0.1 multiply_reduce_fusion
  23.3 0.0 copy-done.2
  23.3 0.2 fusion.4
  23.6 30.5 %psum.7 = f32[2,8]{1,0:T(2,128)S(1)} all-reduce(f32[2,8]{1,0:T(2,128)S(1)} %fusion.4), channel_id=1, replica_groups=mesh['order'=16,'blk'=16] {'blk'}, use_global_device_ids=true, to_apply=%region_2.0 | all-reduce | flops 16 | bytes 128 | tf_op jit(solution)/shard_map/psum | solution.py:34
  54.1 0.1 compare_convert_fusion
  54.2 112.0 %reduce-scatter.2.cloned.1.call-done = f32[768,256]{0,1:T(8,128)} async-done(((f32[12288,256]{0,1:T(8,128)}), f32[768,256]{0,1:T(8,128)}) %reduce-scatter.2.cloned.1.call-update) | async-done | bytes 786448 | tf_op jit(solution)/shard_map/reduce_scatter | solution.py:54
  166.2 2.1 broadcast_multiply_fusion
  168.3 11.3 %copy.13 = f32[768,2,2,8,8]{3,4,2,1,0:T(8,128)} copy(f32[768,2,2,8,8]{0,4,3,2,1:T(8,128)} %broadcast_multiply_fusion) | data formatting | bytes 1572864 | tf_op jit(solution)/shard_map/mul | solution.py:27
  179.6 16.1 %multiply_bitcast_fusion = f32[768,2,2,8,8]{3,4,2,1,0:T(8,128)} fusion(f32[2,8]{1,0:T(2,128)S(1)} %rsqrt_multiply_fusion, f32[768,2,2,8,8]{3,4,2,1,0:T(8,128)} %copy.13, f32[768,8,8,1,1]{2,1,4,3,0:T(8,128)} %copy.18), kind=kOutput, calls=%fused_computation | convolution fusion | flops 19070976 | bytes 1769536 | tf_op jit(solution)/shard_map/dvr,dotrq->dotvq/dot_general | solution.py:28
  195.7 9.9 %copy.15 = f32[768,2,2,8,8]{0,4,3,2,1:T(8,128)} copy(f32[768,2,2,8,8]{3,4,2,1,0:T(8,128)} %multiply_bitcast_fusion) | data formatting | bytes 1572864 | tf_op jit(solution)/shard_map/mul | solution.py:35
  205.6 2.3 copy.16
  207.9 2.5 stack.3
  210.5 144.7 %all_to_all.5 = f32[16,768,2,128]{3,1,2,0:T(8,128)} all-to-all(f32[16,768,2,128]{3,1,2,0:T(8,128)S(1)} %stack.3), channel_id=1, replica_groups=mesh['order'=16,'blk'=16] {'blk'}, dimensions={0} | all-to-all | bytes 25165824 | tf_op jit(solution)/shard_map/all_to_all | solution.py:66
  355.1 10.4 %copy.17 = f32[16,768,2,128]{3,1,0,2:T(8,128)} copy(f32[16,768,2,128]{3,1,2,0:T(8,128)} %all_to_all.5) | data formatting | bytes 25165824 | tf_op jit(solution)/shard_map/all_to_all | solution.py:66
  365.6 10.2 %convolution_bitcast_fusion = f32[2,32,128]{2,1,0:T(8,128)} fusion(f32[12288,2,128]{2,0,1:T(8,128)} %bitcast.19, f32[2,32,12288]{2,1,0:T(8,128)S(1)} %copy-done), kind=kOutput, calls=%fused_computation.1 | convolution fusion | flops 1207959552 | bytes 15761408 | tf_op jit(solution)/shard_map/krl,lkc->krc/dot_general | solution.py:62
  (5 shorter events, 0.0 us)
Async XLA Ops:
  6.5 2.0 copy-start
  6.5 159.7 %reduce-scatter.2.cloned.1.call-start = ((), (), s32[]{:S(2)}) async-start(), calls=%async_computation.2 | async-start | bytes 13369344 | tf_op jit(solution)/shard_map/reduce_scatter | solution.py:54
  8.5 12.5 %copy-start.1 = (f32[768,8,8]{0,2,1:T(8,128)S(1)}, f32[768,8,8]{0,2,1:T(8,128)}, u32[]{:S(2)}) copy-start(f32[768,8,8]{0,2,1:T(8,128)} %param.10) | copy-start | bytes 589828
  8.5 14.8 %copy-start.2 = (s32[2]{0:T(128)S(1)}, s32[2]{0:T(128)}, u32[]{:S(2)}) copy-start(s32[2]{0:T(128)} %param.13) | copy-start | bytes 28
Sparse Core Ops, SparseCore 0:
  21.1 145.0 reduce-scatter.1

commit v2 on v0

--- a/solution.py
+++ b/solution.py
@@ -31,7 +31,7 @@
     squares = jnp.sum(matched_filter_weights * matched_filter_weights, axis=2)
     weights = kept_mask * (2.0 * degrees.astype(jnp.float32) + 1.0)[:, None]
     response = jnp.einsum("lk,ls->ks", weights, squares, precision=highest_degree)
-    response = lax.psum(response, "blk")
+    response = jnp.sum(lax.all_gather(response, "blk"), axis=0)
     scaled = matched_output * (L / jnp.sqrt(response))[None, :, None, :, None]
     return scaled.reshape(blocks, M, 2 * S * SIMS)
 

time: 301 us -> 300 us (level)
  blocking collectives: 30.7 us -> 21.6 us
  waiting for transfers between devices: 187 us -> 196 us
    psum x1 -> x0, blocking collectives: 30.7 us -> none  [finish(): response = lax.psum(response, 'blk')]
    all_gather x0 -> x1, blocking collectives: none -> 21.6 us  [finish(): response = jnp.sum(lax.all_gather(response, 'blk'), axis=0)]
    reduce_scatter x1, waiting for transfers between devices: 112 us -> 121 us  [body(): lax.psum_scatter(partial_running_sum.reshape(blocks * lax.axis_size('blk'...]
where the time goes in v2:
time: 300 us
  waiting for transfers between devices  196 us (65%)
  matrix products  40.3 us (13%)
  local copies, waits for them, and re-layouts  26.6 us (9%)
  blocking collectives  21.6 us (7%)
  between operations  13.4 us (4%)
    reduce_scatter x1, waiting for transfers between devices, body(): lax.psum_scatter(partial_running_sum.reshape(blocks * lax.axis_size('blk'...  121 us
    all_gather x1, waiting for transfers between devices, body(): lax.all_gather(scaled, 'blk', axis=0, tiled=True)  75.3 us
    all_gather x1, blocking collectives, finish(): response = jnp.sum(lax.all_gather(response, 'blk'), axis=0)  21.6 us
    dot_general x1, matrix products, finish(): jnp.einsum('dvr,dotrq->dotvq', matched_filter_weights, masked_values, pre...  16.1 us
    dot_general x1, matrix products, body(): jnp.einsum('krl,krc->lkc', columns, injected, precision=highest_degree)  12.6 us
    mul x1, local copies, waits for them, and re-layouts, finish(): harmonics * kept_mask[:, :, None]  11.3 us
    dot_general x1, matrix products, body(): jnp.einsum('krl,lkc->krc', columns, lax.all_gather(scaled, 'blk', axis=0,...  10.2 us
    mul x1, local copies, waits for them, and re-layouts, finish(): scaled = matched_output * (L / jnp.sqrt(response))[None, :, None, :, None]  9.92 us
  transfers between devices with their start and end apart: 2, of which 2 were waited for; matrix products, arithmetic and copies ran while one was open for 1% of the time, Pallas kernels for 0%

profile of v2, /device:TPU:1, one launch (start us, length us, event | category | flops | bytes accessed | tf_op | source)
XLA Modules:
  0.0 300.2 jit_solution(9863415770965442094)
XLA Ops:
  6.5 0.0 copy-start
  6.5 0.0 reduce-scatter.2.cloned.1.call-start
  6.5 1.2 fusion
  7.7 0.8 copy-done
  8.5 0.0 copy-start.2
  8.5 12.6 %fusion.9 = f32[2,128,12288]{2,1,0:T(8,128)} fusion(f32[2,32,128]{2,1,0:T(8,128)S(1)} %fusion, f32[2,32,12288]{2,1,0:T(8,128)S(1)} %copy-done), kind=kOutput, calls=%fused_computation.21 | convolution fusion | flops 1207959552 | bytes 15761408 | tf_op jit(solution)/shard_map/krl,krc->lkc/dot_general | solution.py:53
  21.1 0.0 reduce-scatter.2.cloned.1.call-update
  21.1 0.0 all-gather.4.cloned.1.call-start
  21.1 0.0 copy-done.1
  21.2 2.3 copy.17
  23.5 0.1 multiply_reduce_fusion
  23.5 0.0 copy-done.2
  23.5 0.2 convolution_bitcast_fusion.1
  23.7 21.6 %all-gather.1 = f32[16,2,8]{2,1,0:T(2,128)S(1)} all-gather(f32[1,2,8]{2,1,0:T(2,128)S(1)} %convolution_bitcast_fusion.1), channel_id=2, replica_groups=mesh['order'=16,'blk'=16] {'blk'}, dimensions={0}, use_global_device_ids=true | all-gather | bytes 1088 | tf_op jit(solution)/shard_map/all_gather | solution.py:34
  45.3 0.1 compare_convert_fusion
  45.4 120.6 %reduce-scatter.2.cloned.1.call-done = f32[768,256]{0,1:T(8,128)} async-done(((f32[12288,256]{0,1:T(8,128)}), f32[768,256]{0,1:T(8,128)}) %reduce-scatter.2.cloned.1.call-update) | async-done | bytes 786448 | tf_op jit(solution)/shard_map/reduce_scatter | solution.py:54
  166.0 2.1 broadcast_multiply_fusion
  168.1 11.3 %copy.13 = f32[768,2,2,8,8]{3,4,2,1,0:T(8,128)} copy(f32[768,2,2,8,8]{0,4,3,2,1:T(8,128)} %broadcast_multiply_fusion) | data formatting | bytes 1572864 | tf_op jit(solution)/shard_map/mul | solution.py:27
  179.4 16.1 %multiply_bitcast_fusion = f32[768,2,2,8,8]{3,4,2,1,0:T(8,128)} fusion(f32[2,8]{1,0:T(2,128)S(1)} %rsqrt_multiply_fusion, f32[768,2,2,8,8]{3,4,2,1,0:T(8,128)} %copy.13, f32[768,8,8,1,1]{2,1,4,3,0:T(8,128)} %copy.17), kind=kOutput, calls=%fused_computation | convolution fusion | flops 19070976 | bytes 1769536 | tf_op jit(solution)/shard_map/dvr,dotrq->dotvq/dot_general | solution.py:28
  195.5 9.9 %copy.15 = f32[768,2,2,8,8]{0,4,3,2,1:T(8,128)} copy(f32[768,2,2,8,8]{3,4,2,1,0:T(8,128)} %multiply_bitcast_fusion) | data formatting | bytes 1572864 | tf_op jit(solution)/shard_map/mul | solution.py:35
  205.4 2.3 copy.16
  207.8 0.0 all-gather.4.cloned.1.call-update
  207.8 75.3 %all-gather.4.cloned.1.call-done = f32[12288,2,128]{2,0,1:T(8,128)} async-done(((f32[768,2,128]{2,0,1:T(8,128)}), f32[12288,2,128]{2,0,1:T(8,128)}) %all-gather.4.cloned.1.call-update) | async-done | bytes 12582928 | tf_op jit(solution)/shard_map/all_gather | solution.py:65
  283.1 10.2 %convolution_bitcast_fusion = f32[2,32,128]{2,1,0:T(8,128)} fusion(f32[12288,2,128]{2,0,1:T(8,128)} %all-gather.4.cloned.1.call-done, f32[2,32,12288]{2,1,0:T(8,128)S(1)} %copy-done), kind=kOutput, calls=%fused_computation.1 | convolution fusion | flops 1207959552 | bytes 15761408 | tf_op jit(solution)/shard_map/krl,lkc->krc/dot_general | solution.py:62
  (6 shorter events, 0.0 us)
Async XLA Ops:
  6.5 2.0 copy-start
  6.5 159.5 %reduce-scatter.2.cloned.1.call-start = ((), (), s32[]{:S(2)}) async-start(), calls=%async_computation.1 | async-start | bytes 13369344 | tf_op jit(solution)/shard_map/reduce_scatter | solution.py:54
  8.5 12.6 %copy-start.1 = (f32[768,8,8]{0,2,1:T(8,128)S(1)}, f32[768,8,8]{0,2,1:T(8,128)}, u32[]{:S(2)}) copy-start(f32[768,8,8]{0,2,1:T(8,128)} %param.10) | copy-start | bytes 589828
  8.5 15.0 %copy-start.2 = (s32[2]{0:T(128)S(1)}, s32[2]{0:T(128)}, u32[]{:S(2)}) copy-start(s32[2]{0:T(128)} %param.13) | copy-start | bytes 28
  21.1 262.0 %all-gather.4.cloned.1.call-start = ((), (), s32[]{:S(2)}) async-start(), calls=%async_computation.2 | async-start | bytes 13369344 | tf_op jit(solution)/shard_map/all_gather | solution.py:65
Sparse Core Ops, SparseCore 0:
  21.2 144.7 reduce-scatter.1
  207.9 75.1 all-gather.3
